TPU v7x, 512 devices: a whole 4x4x16 slice. The times are simulated.
512 devices in a mesh: depth: 8 (over x, core), strip: 64 (over y, z).
Axes of the slice: x: 4, y: 4, z: 16, core: 2. Of those that a mesh axis runs over, the one named last changes fastest.
Arguments:
- surface: float32 [2, 4, 1024, 1024], P(None, None, 'strip'), may hold values from -6 to 6
- velocity_class: int32 [8, 1024, 1024], P('depth', 'strip'), may hold values from 0 to 7
- table: float32 [2, 8, 2, 10], replicated, may hold values from -2 to 2
Outputs:
- image: float32 [8, 1024, 1024], P('depth', 'strip')
All inputs are finite; a program needn't handle non-finite values.
Results may differ from a plain program's by a relative error of at most 0.00017.
Values sent between devices are 32-bit elements; how exact they have to be, the bound alone decides.
No kernel may reach another device: no remote copies, remote signals or barrier semaphores. Data moves between devices by JAX's collectives and lax.ppermute only.
A program may use at most 64 MiB of HBM per device.

v0:
```python
import jax
import jax.numpy as jnp
from jax import lax
from jax.sharding import PartitionSpec as P

PASSES = 9
CLASSES = 8


def extended(shard, sides, width):
    for axis, dim in sides:
        devices, length = (lax.axis_size(axis), shard.shape[dim])
        up = [(i, (i + 1) % devices) for i in range(devices - 1)]
        down = [(j, i) for i, j in up]
        last = lax.slice_in_dim(shard, length - width, length, axis=dim)
        initial = lax.slice_in_dim(shard, 0, width, axis=dim)
        before = lax.ppermute(last, axis, up)
        after = lax.ppermute(initial, axis, down)
        shard = jnp.concatenate([before, shard, after], axis=dim)
    return shard


def mcclellan(field):
    lead = [(0, 0)] * (field.ndim - 2)
    padded = jnp.pad(field, lead + [(1, 1), (1, 1)])
    beside = (
        padded[..., 2:, 1:-1]
        + padded[..., :-2, 1:-1]
        + padded[..., 1:-1, 2:]
        + padded[..., 1:-1, :-2]
    )
    corners = (
        padded[..., 2:, 2:] + padded[..., 2:, :-2] + padded[..., :-2, 2:] + padded[..., :-2, :-2]
    )
    return -0.5 * field + 0.25 * beside + 0.125 * corners


def weigh(result, field, real_part, imag_part):
    return jnp.stack(
        [
            result[:, 0] + (real_part * field[:, 0] - imag_part * field[:, 1]),
            result[:, 1] + (real_part * field[:, 1] + imag_part * field[:, 0]),
            result[:, 2] + (real_part * field[:, 2] + imag_part * field[:, 3]),
            result[:, 3] + (real_part * field[:, 3] - imag_part * field[:, 2]),
        ],
        axis=1,
    )


def correlate(fields):
    total = jnp.zeros(fields.shape[2:], jnp.float32)
    for freq_index in range(fields.shape[0]):
        total = total + (
            fields[freq_index, 0] * fields[freq_index, 2]
            + fields[freq_index, 1] * fields[freq_index, 3]
        )
    return total


def tile_halo(sending, rim_width):
    return extended(sending, (("depth", 4), ("strip", 3)), rim_width)


def clip_domain(field, rim_width):
    row_count = field.shape[-2] - 2 * rim_width
    row_ids = (
        lax.axis_index("strip") * row_count
        - rim_width
        + jnp.arange(field.shape[-2], dtype=jnp.int32)
    )
    keep = ((row_ids >= 0) & (row_ids < row_count * lax.axis_size("strip")))[:, None]
    col_count = field.shape[-1] - 2 * rim_width
    col_ids = (
        lax.axis_index("depth") * col_count
        - rim_width
        + jnp.arange(field.shape[-1], dtype=jnp.int32)
    )
    keep = keep & ((col_ids >= 0) & (col_ids < col_count * lax.axis_size("depth")))[None, :]
    return jnp.where(keep, field, 0.0)


def chebyshev(fields, onehot, table_part, rim_width, widen):
    row_count = fields.shape[-2]
    col_count = fields.shape[-1]

    def own_cells(field):
        inner = field[..., rim_width : rim_width + row_count, :]
        inner = inner[..., rim_width : rim_width + col_count]
        return inner

    def coefficients(degree):
        pair = jnp.einsum(
            "cij,fcp->fpij", onehot, table_part[:, :, :, degree], precision=lax.Precision.HIGHEST
        )
        return (pair[:, 0], pair[:, 1])

    real_part, imag_part = coefficients(0)
    result = weigh(jnp.zeros_like(fields), fields, real_part, imag_part)
    previous = fields
    current = fields
    for block_index in range(PASSES // rim_width):
        sending = current[None] if block_index == 0 else jnp.stack([previous, current])
        widened = widen(sending, rim_width)
        wide_prev = widened[0]
        wide_curr = widened[-1]
        for inner_pass in range(rim_width):
            degree = block_index * rim_width + inner_pass
            if degree == 0:
                following = mcclellan(wide_curr)
            else:
                following = 2.0 * mcclellan(wide_curr) - wide_prev
            following = clip_domain(following, rim_width)
            wide_prev, wide_curr = (wide_curr, following)
            real_part, imag_part = coefficients(degree + 1)
            result = weigh(result, own_cells(wide_curr), real_part, imag_part)
        previous = own_cells(wide_prev)
        current = own_cells(wide_curr)
    return result


def body(surface, velocity_class, table):
    classes = jnp.arange(CLASSES, dtype=jnp.int32)
    rim_width = 3
    velocity = lax.all_to_all(velocity_class, "depth", split_axis=2, concat_axis=0, tiled=True)
    col_count = velocity.shape[2]
    fields = lax.dynamic_slice_in_dim(surface, lax.axis_index("depth") * col_count, col_count, 3)

    def descend(level_index, state_pair):
        level_fields, image = state_pair
        classes_here = lax.dynamic_index_in_dim(velocity, level_index, 0, keepdims=False)
        onehot = (classes_here[None] == classes[:, None, None]).astype(jnp.float32)
        level_fields = chebyshev(level_fields, onehot, table, rim_width, tile_halo)
        image = lax.dynamic_update_index_in_dim(image, correlate(level_fields), level_index, 0)
        return (level_fields, image)

    initial = (fields, jnp.zeros((velocity.shape[0], velocity.shape[1], col_count), jnp.float32))
    fields, image = lax.fori_loop(0, velocity.shape[0], descend, initial)
    return lax.all_to_all(image, "depth", split_axis=0, concat_axis=2, tiled=True)


def solution(mesh):
    in_specs = (P(None, None, "strip", None), P("depth", "strip", None), P())
    out_specs = P("depth", "strip", None)
    return jax.shard_map(body, mesh=mesh, in_specs=in_specs, out_specs=out_specs, check_vma=False)
```

profile of v0, /device:TPU:24, one launch (start us, length us, event | category | flops | bytes accessed | tf_op | source)
XLA Modules:
  0.0 554.1 jit_solution(4502682108848891029)
XLA Ops:
  16.5 522.7 %while.19 = (s32[]{:T(128)}, f32[2,4,16,128]{3,1,0,2:T(4,128)S(1)}, f32[8,16,128]{2,1,0:T(8,128)S(1)}, s32[8,16,128]{2,0,1:T(8,128)S(1)}, f32[2,8,2,10]{1,2,0,3:...) while((s32[]{:T(128)}, f32[2,4,16,128]{3,1,0,2:T(4,128)S(1)}, ...), condition=%wide.region_1.2_spmd.clone, body=%wide.region_0.1_spmd.clone.sunk | while | flops 12695103 | bytes 9011121 | solution.py:137
  22.6 11.6 %collective-permute-start.2 = (f32[1,2,4,3,134]{4,2,1,3,0:T(4,128)S(1)}, f32[1,2,4,3,134]{4,2,1,3,0:T(4,128)S(1)}, u32[]{:S(2)}, u32[]{:S(2)}) collective-permute-start(f32[1,2,4,3,134]{4,2,1,3,0:T(4,128)S(1)} %get-tuple-element.279), channel_id=1, source_target_pairs={{1,0},{2,1},{3,2},{4,3},{5,4},{6,5},{7,6},{8,7},{9,8},{10,9},{11,1... | collective-permute-start | bytes 38600 | tf_op jit(solution)/shard_map/while/body/eval_jaxpr/ppermute | solution.py:18
  36.2 5.8 %collective-permute-done.3 = f32[1,2,4,3,134]{4,2,1,3,0:T(4,128)S(1)} collective-permute-done((f32[1,2,4,3,134]{4,2,1,3,0:T(4,128)S(1)}, f32[1,2,4,3,134]{4,2,1,3,0:T(4,128)S(1)}, u32[]{:S(2)}, u32[]{:S(2)}) %collective-permute-start.3) | collective-permute-done | bytes 12896 | tf_op jit(solution)/shard_map/while/body/eval_jaxpr/ppermute | solution.py:17
  64.2 5.2 collective-permute-start.9
  87.1 5.9 %collective-permute-start.1 = (f32[1,2,4,16,3]{4,2,1,3,0:T(4,128)S(1)}, f32[1,2,4,16,3]{4,2,1,3,0:T(4,128)S(1)}, u32[]{:S(2)}, u32[]{:S(2)}) collective-permute-start(f32[1,2,4,16,3]{4,2,1,3,0:T(4,128)S(1)} %get-tuple-element.278), channel_id=1, source_target_pairs={{0,64},{64,128},{128,192},{192,256},{256,320},{320,384},{384,448},... | collective-permute-start | bytes 4616 | tf_op jit(solution)/shard_map/while/body/eval_jaxpr/ppermute | solution.py:17
  128.3 5.9 %collective-permute-start.9 = (f32[2,2,4,16,3]{4,2,1,3,0:T(4,128)S(1)}, f32[2,2,4,16,3]{4,2,1,3,0:T(4,128)S(1)}, u32[]{:S(2)}, u32[]{:S(2)}) collective-permute-start(f32[2,2,4,16,3]{4,2,1,3,0:T(4,128)S(1)} %get-tuple-element.288), channel_id=1, source_target_pairs={{0,64},{64,128},{128,192},{192,256},{256,320},{320,384},{384,448},... | collective-permute-start | bytes 9224 | tf_op jit(solution)/shard_map/while/body/eval_jaxpr/ppermute | solution.py:17
  151.9 5.9 %collective-permute-start.1 = (f32[1,2,4,16,3]{4,2,1,3,0:T(4,128)S(1)}, f32[1,2,4,16,3]{4,2,1,3,0:T(4,128)S(1)}, u32[]{:S(2)}, u32[]{:S(2)}) collective-permute-start(f32[1,2,4,16,3]{4,2,1,3,0:T(4,128)S(1)} %get-tuple-element.278), channel_id=1, source_target_pairs={{0,64},{64,128},{128,192},{192,256},{256,320},{320,384},{384,448},... | collective-permute-start | bytes 4616 | tf_op jit(solution)/shard_map/while/body/eval_jaxpr/ppermute | solution.py:17
  173.2 5.0 collective-permute-start.5
  193.1 5.9 %collective-permute-start.9 = (f32[2,2,4,16,3]{4,2,1,3,0:T(4,128)S(1)}, f32[2,2,4,16,3]{4,2,1,3,0:T(4,128)S(1)}, u32[]{:S(2)}, u32[]{:S(2)}) collective-permute-start(f32[2,2,4,16,3]{4,2,1,3,0:T(4,128)S(1)} %get-tuple-element.288), channel_id=1, source_target_pairs={{0,64},{64,128},{128,192},{192,256},{256,320},{320,384},{384,448},... | collective-permute-start | bytes 9224 | tf_op jit(solution)/shard_map/while/body/eval_jaxpr/ppermute | solution.py:17
  216.7 5.9 %collective-permute-start.1 = (f32[1,2,4,16,3]{4,2,1,3,0:T(4,128)S(1)}, f32[1,2,4,16,3]{4,2,1,3,0:T(4,128)S(1)}, u32[]{:S(2)}, u32[]{:S(2)}) collective-permute-start(f32[1,2,4,16,3]{4,2,1,3,0:T(4,128)S(1)} %get-tuple-element.278), channel_id=1, source_target_pairs={{0,64},{64,128},{128,192},{192,256},{256,320},{320,384},{384,448},... | collective-permute-start | bytes 4616 | tf_op jit(solution)/shard_map/while/body/eval_jaxpr/ppermute | solution.py:17
  238.0 5.0 collective-permute-start.5
  257.9 5.9 %collective-permute-start.9 = (f32[2,2,4,16,3]{4,2,1,3,0:T(4,128)S(1)}, f32[2,2,4,16,3]{4,2,1,3,0:T(4,128)S(1)}, u32[]{:S(2)}, u32[]{:S(2)}) collective-permute-start(f32[2,2,4,16,3]{4,2,1,3,0:T(4,128)S(1)} %get-tuple-element.288), channel_id=1, source_target_pairs={{0,64},{64,128},{128,192},{192,256},{256,320},{320,384},{384,448},... | collective-permute-start | bytes 9224 | tf_op jit(solution)/shard_map/while/body/eval_jaxpr/ppermute | solution.py:17
  281.5 5.9 %collective-permute-start.1 = (f32[1,2,4,16,3]{4,2,1,3,0:T(4,128)S(1)}, f32[1,2,4,16,3]{4,2,1,3,0:T(4,128)S(1)}, u32[]{:S(2)}, u32[]{:S(2)}) collective-permute-start(f32[1,2,4,16,3]{4,2,1,3,0:T(4,128)S(1)} %get-tuple-element.278), channel_id=1, source_target_pairs={{0,64},{64,128},{128,192},{192,256},{256,320},{320,384},{384,448},... | collective-permute-start | bytes 4616 | tf_op jit(solution)/shard_map/while/body/eval_jaxpr/ppermute | solution.py:17
  302.8 5.0 collective-permute-start.5
  322.7 5.9 %collective-permute-start.9 = (f32[2,2,4,16,3]{4,2,1,3,0:T(4,128)S(1)}, f32[2,2,4,16,3]{4,2,1,3,0:T(4,128)S(1)}, u32[]{:S(2)}, u32[]{:S(2)}) collective-permute-start(f32[2,2,4,16,3]{4,2,1,3,0:T(4,128)S(1)} %get-tuple-element.288), channel_id=1, source_target_pairs={{0,64},{64,128},{128,192},{192,256},{256,320},{320,384},{384,448},... | collective-permute-start | bytes 9224 | tf_op jit(solution)/shard_map/while/body/eval_jaxpr/ppermute | solution.py:17
  346.3 5.9 %collective-permute-start.1 = (f32[1,2,4,16,3]{4,2,1,3,0:T(4,128)S(1)}, f32[1,2,4,16,3]{4,2,1,3,0:T(4,128)S(1)}, u32[]{:S(2)}, u32[]{:S(2)}) collective-permute-start(f32[1,2,4,16,3]{4,2,1,3,0:T(4,128)S(1)} %get-tuple-element.278), channel_id=1, source_target_pairs={{0,64},{64,128},{128,192},{192,256},{256,320},{320,384},{384,448},... | collective-permute-start | bytes 4616 | tf_op jit(solution)/shard_map/while/body/eval_jaxpr/ppermute | solution.py:17
  367.6 5.0 collective-permute-start.5
  387.5 5.9 %collective-permute-start.9 = (f32[2,2,4,16,3]{4,2,1,3,0:T(4,128)S(1)}, f32[2,2,4,16,3]{4,2,1,3,0:T(4,128)S(1)}, u32[]{:S(2)}, u32[]{:S(2)}) collective-permute-start(f32[2,2,4,16,3]{4,2,1,3,0:T(4,128)S(1)} %get-tuple-element.288), channel_id=1, source_target_pairs={{0,64},{64,128},{128,192},{192,256},{256,320},{320,384},{384,448},... | collective-permute-start | bytes 9224 | tf_op jit(solution)/shard_map/while/body/eval_jaxpr/ppermute | solution.py:17
  411.0 5.9 %collective-permute-start.1 = (f32[1,2,4,16,3]{4,2,1,3,0:T(4,128)S(1)}, f32[1,2,4,16,3]{4,2,1,3,0:T(4,128)S(1)}, u32[]{:S(2)}, u32[]{:S(2)}) collective-permute-start(f32[1,2,4,16,3]{4,2,1,3,0:T(4,128)S(1)} %get-tuple-element.278), channel_id=1, source_target_pairs={{0,64},{64,128},{128,192},{192,256},{256,320},{320,384},{384,448},... | collective-permute-start | bytes 4616 | tf_op jit(solution)/shard_map/while/body/eval_jaxpr/ppermute | solution.py:17
  452.3 5.9 %collective-permute-start.9 = (f32[2,2,4,16,3]{4,2,1,3,0:T(4,128)S(1)}, f32[2,2,4,16,3]{4,2,1,3,0:T(4,128)S(1)}, u32[]{:S(2)}, u32[]{:S(2)}) collective-permute-start(f32[2,2,4,16,3]{4,2,1,3,0:T(4,128)S(1)} %get-tuple-element.288), channel_id=1, source_target_pairs={{0,64},{64,128},{128,192},{192,256},{256,320},{320,384},{384,448},... | collective-permute-start | bytes 9224 | tf_op jit(solution)/shard_map/while/body/eval_jaxpr/ppermute | solution.py:17
  475.8 5.9 %collective-permute-start.1 = (f32[1,2,4,16,3]{4,2,1,3,0:T(4,128)S(1)}, f32[1,2,4,16,3]{4,2,1,3,0:T(4,128)S(1)}, u32[]{:S(2)}, u32[]{:S(2)}) collective-permute-start(f32[1,2,4,16,3]{4,2,1,3,0:T(4,128)S(1)} %get-tuple-element.278), channel_id=1, source_target_pairs={{0,64},{64,128},{128,192},{192,256},{256,320},{320,384},{384,448},... | collective-permute-start | bytes 4616 | tf_op jit(solution)/shard_map/while/body/eval_jaxpr/ppermute | solution.py:17
  497.2 5.0 collective-permute-start.5
  517.1 5.9 %collective-permute-start.9 = (f32[2,2,4,16,3]{4,2,1,3,0:T(4,128)S(1)}, f32[2,2,4,16,3]{4,2,1,3,0:T(4,128)S(1)}, u32[]{:S(2)}, u32[]{:S(2)}) collective-permute-start(f32[2,2,4,16,3]{4,2,1,3,0:T(4,128)S(1)} %get-tuple-element.288), channel_id=1, source_target_pairs={{0,64},{64,128},{128,192},{192,256},{256,320},{320,384},{384,448},... | collective-permute-start | bytes 9224 | tf_op jit(solution)/shard_map/while/body/eval_jaxpr/ppermute | solution.py:17
  539.2 14.2 %all_to_all.36 = f32[8,16,128]{2,1,0:T(8,128)S(1)} all-to-all(f32[8,16,128]{2,1,0:T(8,128)S(1)} %get-tuple-element.180), channel_id=1, replica_groups=mesh['depth'=8,'strip'=64] {'depth'}, dimensions={0} | all-to-all | bytes 131072 | tf_op jit(solution)/shard_map/all_to_all | solution.py:138
  (540 shorter events, 405.6 us)
Async XLA Ops:
  4.6 9.9 %all-to-all-start = ((s32[8,1,2048]{2,1,0:T(1,128)}), s32[8,1,2048]{2,1,0:T(1,128)S(1)}, u32[]{:S(2)}, u32[]{:S(2)}) async-start(s32[8,1,2048]{2,1,0:T(1,128)} %reshape.214), calls=%async_computation | async-start | bytes 131072 | tf_op jit(solution)/shard_map/all_to_all | solution.py:124
  22.6 13.6 %collective-permute-start.2 = (f32[1,2,4,3,134]{4,2,1,3,0:T(4,128)S(1)}, f32[1,2,4,3,134]{4,2,1,3,0:T(4,128)S(1)}, u32[]{:S(2)}, u32[]{:S(2)}) collective-permute-start(f32[1,2,4,3,134]{4,2,1,3,0:T(4,128)S(1)} %get-tuple-element.279), channel_id=1, source_target_pairs={{1,0},{2,1},{3,2},{4,3},{5,4},{6,5},{7,6},{8,7},{9,8},{10,9},{11,1... | collective-permute-start | bytes 38600 | tf_op jit(solution)/shard_map/while/body/eval_jaxpr/ppermute | solution.py:18
  52.3 8.1 %collective-permute-start.7 = (f32[2,2,4,3,134]{4,2,1,3,0:T(4,128)S(1)}, f32[2,2,4,3,134]{4,2,1,3,0:T(4,128)S(1)}, u32[]{:S(2)}, u32[]{:S(2)}) collective-permute-start(f32[2,2,4,3,134]{4,2,1,3,0:T(4,128)S(1)} %get-tuple-element.286), channel_id=1, source_target_pairs={{0,1},{1,2},{2,3},{3,4},{4,5},{5,6},{6,7},{7,8},{8,9},{9,10},{10,1... | collective-permute-start | bytes 77192 | tf_op jit(solution)/shard_map/while/body/eval_jaxpr/ppermute | solution.py:17
  72.4 8.1 %collective-permute-start.11 = (f32[2,2,4,3,134]{4,2,1,3,0:T(4,128)S(1)}, f32[2,2,4,3,134]{4,2,1,3,0:T(4,128)S(1)}, u32[]{:S(2)}, u32[]{:S(2)}) collective-permute-start(f32[2,2,4,3,134]{4,2,1,3,0:T(4,128)S(1)} %get-tuple-element.290), channel_id=1, source_target_pairs={{0,1},{1,2},{2,3},{3,4},{4,5},{5,6},{6,7},{7,8},{8,9},{9,10},{10,1... | collective-permute-start | bytes 77192 | tf_op jit(solution)/shard_map/while/body/eval_jaxpr/ppermute | solution.py:17
  85.8 8.5 %collective-permute-start = (f32[1,2,4,16,3]{4,2,1,3,0:T(4,128)S(1)}, f32[1,2,4,16,3]{4,2,1,3,0:T(4,128)S(1)}, u32[]{:S(2)}, u32[]{:S(2)}) collective-permute-start(f32[1,2,4,16,3]{4,2,1,3,0:T(4,128)S(1)} %get-tuple-element.277), channel_id=1, source_target_pairs={{64,0},{128,64},{192,128},{256,192},{320,256},{384,320},{448,384},... | collective-permute-start | bytes 4616 | tf_op jit(solution)/shard_map/while/body/eval_jaxpr/ppermute | solution.py:18
  116.5 8.1 %collective-permute-start.7 = (f32[2,2,4,3,134]{4,2,1,3,0:T(4,128)S(1)}, f32[2,2,4,3,134]{4,2,1,3,0:T(4,128)S(1)}, u32[]{:S(2)}, u32[]{:S(2)}) collective-permute-start(f32[2,2,4,3,134]{4,2,1,3,0:T(4,128)S(1)} %get-tuple-element.286), channel_id=1, source_target_pairs={{0,1},{1,2},{2,3},{3,4},{4,5},{5,6},{6,7},{7,8},{8,9},{9,10},{10,1... | collective-permute-start | bytes 77192 | tf_op jit(solution)/shard_map/while/body/eval_jaxpr/ppermute | solution.py:17
  137.2 8.1 %collective-permute-start.11 = (f32[2,2,4,3,134]{4,2,1,3,0:T(4,128)S(1)}, f32[2,2,4,3,134]{4,2,1,3,0:T(4,128)S(1)}, u32[]{:S(2)}, u32[]{:S(2)}) collective-permute-start(f32[2,2,4,3,134]{4,2,1,3,0:T(4,128)S(1)} %get-tuple-element.290), channel_id=1, source_target_pairs={{0,1},{1,2},{2,3},{3,4},{4,5},{5,6},{6,7},{7,8},{8,9},{9,10},{10,1... | collective-permute-start | bytes 77192 | tf_op jit(solution)/shard_map/while/body/eval_jaxpr/ppermute | solution.py:17
  150.6 8.5 %collective-permute-start = (f32[1,2,4,16,3]{4,2,1,3,0:T(4,128)S(1)}, f32[1,2,4,16,3]{4,2,1,3,0:T(4,128)S(1)}, u32[]{:S(2)}, u32[]{:S(2)}) collective-permute-start(f32[1,2,4,16,3]{4,2,1,3,0:T(4,128)S(1)} %get-tuple-element.277), channel_id=1, source_target_pairs={{64,0},{128,64},{192,128},{256,192},{320,256},{384,320},{448,384},... | collective-permute-start | bytes 4616 | tf_op jit(solution)/shard_map/while/body/eval_jaxpr/ppermute | solution.py:18
  181.3 8.1 %collective-permute-start.7 = (f32[2,2,4,3,134]{4,2,1,3,0:T(4,128)S(1)}, f32[2,2,4,3,134]{4,2,1,3,0:T(4,128)S(1)}, u32[]{:S(2)}, u32[]{:S(2)}) collective-permute-start(f32[2,2,4,3,134]{4,2,1,3,0:T(4,128)S(1)} %get-tuple-element.286), channel_id=1, source_target_pairs={{0,1},{1,2},{2,3},{3,4},{4,5},{5,6},{6,7},{7,8},{8,9},{9,10},{10,1... | collective-permute-start | bytes 77192 | tf_op jit(solution)/shard_map/while/body/eval_jaxpr/ppermute | solution.py:17
  202.0 8.1 %collective-permute-start.11 = (f32[2,2,4,3,134]{4,2,1,3,0:T(4,128)S(1)}, f32[2,2,4,3,134]{4,2,1,3,0:T(4,128)S(1)}, u32[]{:S(2)}, u32[]{:S(2)}) collective-permute-start(f32[2,2,4,3,134]{4,2,1,3,0:T(4,128)S(1)} %get-tuple-element.290), channel_id=1, source_target_pairs={{0,1},{1,2},{2,3},{3,4},{4,5},{5,6},{6,7},{7,8},{8,9},{9,10},{10,1... | collective-permute-start | bytes 77192 | tf_op jit(solution)/shard_map/while/body/eval_jaxpr/ppermute | solution.py:17
  215.4 8.5 %collective-permute-start = (f32[1,2,4,16,3]{4,2,1,3,0:T(4,128)S(1)}, f32[1,2,4,16,3]{4,2,1,3,0:T(4,128)S(1)}, u32[]{:S(2)}, u32[]{:S(2)}) collective-permute-start(f32[1,2,4,16,3]{4,2,1,3,0:T(4,128)S(1)} %get-tuple-element.277), channel_id=1, source_target_pairs={{64,0},{128,64},{192,128},{256,192},{320,256},{384,320},{448,384},... | collective-permute-start | bytes 4616 | tf_op jit(solution)/shard_map/while/body/eval_jaxpr/ppermute | solution.py:18
  246.1 8.1 %collective-permute-start.7 = (f32[2,2,4,3,134]{4,2,1,3,0:T(4,128)S(1)}, f32[2,2,4,3,134]{4,2,1,3,0:T(4,128)S(1)}, u32[]{:S(2)}, u32[]{:S(2)}) collective-permute-start(f32[2,2,4,3,134]{4,2,1,3,0:T(4,128)S(1)} %get-tuple-element.286), channel_id=1, source_target_pairs={{0,1},{1,2},{2,3},{3,4},{4,5},{5,6},{6,7},{7,8},{8,9},{9,10},{10,1... | collective-permute-start | bytes 77192 | tf_op jit(solution)/shard_map/while/body/eval_jaxpr/ppermute | solution.py:17
  266.8 8.1 %collective-permute-start.11 = (f32[2,2,4,3,134]{4,2,1,3,0:T(4,128)S(1)}, f32[2,2,4,3,134]{4,2,1,3,0:T(4,128)S(1)}, u32[]{:S(2)}, u32[]{:S(2)}) collective-permute-start(f32[2,2,4,3,134]{4,2,1,3,0:T(4,128)S(1)} %get-tuple-element.290), channel_id=1, source_target_pairs={{0,1},{1,2},{2,3},{3,4},{4,5},{5,6},{6,7},{7,8},{8,9},{9,10},{10,1... | collective-permute-start | bytes 77192 | tf_op jit(solution)/shard_map/while/body/eval_jaxpr/ppermute | solution.py:17
  280.2 8.5 %collective-permute-start = (f32[1,2,4,16,3]{4,2,1,3,0:T(4,128)S(1)}, f32[1,2,4,16,3]{4,2,1,3,0:T(4,128)S(1)}, u32[]{:S(2)}, u32[]{:S(2)}) collective-permute-start(f32[1,2,4,16,3]{4,2,1,3,0:T(4,128)S(1)} %get-tuple-element.277), channel_id=1, source_target_pairs={{64,0},{128,64},{192,128},{256,192},{320,256},{384,320},{448,384},... | collective-permute-start | bytes 4616 | tf_op jit(solution)/shard_map/while/body/eval_jaxpr/ppermute | solution.py:18
  310.9 8.1 %collective-permute-start.7 = (f32[2,2,4,3,134]{4,2,1,3,0:T(4,128)S(1)}, f32[2,2,4,3,134]{4,2,1,3,0:T(4,128)S(1)}, u32[]{:S(2)}, u32[]{:S(2)}) collective-permute-start(f32[2,2,4,3,134]{4,2,1,3,0:T(4,128)S(1)} %get-tuple-element.286), channel_id=1, source_target_pairs={{0,1},{1,2},{2,3},{3,4},{4,5},{5,6},{6,7},{7,8},{8,9},{9,10},{10,1... | collective-permute-start | bytes 77192 | tf_op jit(solution)/shard_map/while/body/eval_jaxpr/ppermute | solution.py:17
  331.6 8.1 %collective-permute-start.11 = (f32[2,2,4,3,134]{4,2,1,3,0:T(4,128)S(1)}, f32[2,2,4,3,134]{4,2,1,3,0:T(4,128)S(1)}, u32[]{:S(2)}, u32[]{:S(2)}) collective-permute-start(f32[2,2,4,3,134]{4,2,1,3,0:T(4,128)S(1)} %get-tuple-element.290), channel_id=1, source_target_pairs={{0,1},{1,2},{2,3},{3,4},{4,5},{5,6},{6,7},{7,8},{8,9},{9,10},{10,1... | collective-permute-start | bytes 77192 | tf_op jit(solution)/shard_map/while/body/eval_jaxpr/ppermute | solution.py:17
  345.0 8.5 %collective-permute-start = (f32[1,2,4,16,3]{4,2,1,3,0:T(4,128)S(1)}, f32[1,2,4,16,3]{4,2,1,3,0:T(4,128)S(1)}, u32[]{:S(2)}, u32[]{:S(2)}) collective-permute-start(f32[1,2,4,16,3]{4,2,1,3,0:T(4,128)S(1)} %get-tuple-element.277), channel_id=1, source_target_pairs={{64,0},{128,64},{192,128},{256,192},{320,256},{384,320},{448,384},... | collective-permute-start | bytes 4616 | tf_op jit(solution)/shard_map/while/body/eval_jaxpr/ppermute | solution.py:18
  396.4 8.1 %collective-permute-start.11 = (f32[2,2,4,3,134]{4,2,1,3,0:T(4,128)S(1)}, f32[2,2,4,3,134]{4,2,1,3,0:T(4,128)S(1)}, u32[]{:S(2)}, u32[]{:S(2)}) collective-permute-start(f32[2,2,4,3,134]{4,2,1,3,0:T(4,128)S(1)} %get-tuple-element.290), channel_id=1, source_target_pairs={{0,1},{1,2},{2,3},{3,4},{4,5},{5,6},{6,7},{7,8},{8,9},{9,10},{10,1... | collective-permute-start | bytes 77192 | tf_op jit(solution)/shard_map/while/body/eval_jaxpr/ppermute | solution.py:17
  409.7 8.5 %collective-permute-start = (f32[1,2,4,16,3]{4,2,1,3,0:T(4,128)S(1)}, f32[1,2,4,16,3]{4,2,1,3,0:T(4,128)S(1)}, u32[]{:S(2)}, u32[]{:S(2)}) collective-permute-start(f32[1,2,4,16,3]{4,2,1,3,0:T(4,128)S(1)} %get-tuple-element.277), channel_id=1, source_target_pairs={{64,0},{128,64},{192,128},{256,192},{320,256},{384,320},{448,384},... | collective-permute-start | bytes 4616 | tf_op jit(solution)/shard_map/while/body/eval_jaxpr/ppermute | solution.py:18
  440.4 8.1 %collective-permute-start.7 = (f32[2,2,4,3,134]{4,2,1,3,0:T(4,128)S(1)}, f32[2,2,4,3,134]{4,2,1,3,0:T(4,128)S(1)}, u32[]{:S(2)}, u32[]{:S(2)}) collective-permute-start(f32[2,2,4,3,134]{4,2,1,3,0:T(4,128)S(1)} %get-tuple-element.286), channel_id=1, source_target_pairs={{0,1},{1,2},{2,3},{3,4},{4,5},{5,6},{6,7},{7,8},{8,9},{9,10},{10,1... | collective-permute-start | bytes 77192 | tf_op jit(solution)/shard_map/while/body/eval_jaxpr/ppermute | solution.py:17
  461.2 8.1 %collective-permute-start.11 = (f32[2,2,4,3,134]{4,2,1,3,0:T(4,128)S(1)}, f32[2,2,4,3,134]{4,2,1,3,0:T(4,128)S(1)}, u32[]{:S(2)}, u32[]{:S(2)}) collective-permute-start(f32[2,2,4,3,134]{4,2,1,3,0:T(4,128)S(1)} %get-tuple-element.290), channel_id=1, source_target_pairs={{0,1},{1,2},{2,3},{3,4},{4,5},{5,6},{6,7},{7,8},{8,9},{9,10},{10,1... | collective-permute-start | bytes 77192 | tf_op jit(solution)/shard_map/while/body/eval_jaxpr/ppermute | solution.py:17
  474.5 8.5 %collective-permute-start = (f32[1,2,4,16,3]{4,2,1,3,0:T(4,128)S(1)}, f32[1,2,4,16,3]{4,2,1,3,0:T(4,128)S(1)}, u32[]{:S(2)}, u32[]{:S(2)}) collective-permute-start(f32[1,2,4,16,3]{4,2,1,3,0:T(4,128)S(1)} %get-tuple-element.277), channel_id=1, source_target_pairs={{64,0},{128,64},{192,128},{256,192},{320,256},{384,320},{448,384},... | collective-permute-start | bytes 4616 | tf_op jit(solution)/shard_map/while/body/eval_jaxpr/ppermute | solution.py:18
  505.2 8.1 %collective-permute-start.7 = (f32[2,2,4,3,134]{4,2,1,3,0:T(4,128)S(1)}, f32[2,2,4,3,134]{4,2,1,3,0:T(4,128)S(1)}, u32[]{:S(2)}, u32[]{:S(2)}) collective-permute-start(f32[2,2,4,3,134]{4,2,1,3,0:T(4,128)S(1)} %get-tuple-element.286), channel_id=1, source_target_pairs={{0,1},{1,2},{2,3},{3,4},{4,5},{5,6},{6,7},{7,8},{8,9},{9,10},{10,1... | collective-permute-start | bytes 77192 | tf_op jit(solution)/shard_map/while/body/eval_jaxpr/ppermute | solution.py:17
  526.0 8.1 %collective-permute-start.11 = (f32[2,2,4,3,134]{4,2,1,3,0:T(4,128)S(1)}, f32[2,2,4,3,134]{4,2,1,3,0:T(4,128)S(1)}, u32[]{:S(2)}, u32[]{:S(2)}) collective-permute-start(f32[2,2,4,3,134]{4,2,1,3,0:T(4,128)S(1)} %get-tuple-element.290), channel_id=1, source_target_pairs={{0,1},{1,2},{2,3},{3,4},{4,5},{5,6},{6,7},{7,8},{8,9},{9,10},{10,1... | collective-permute-start | bytes 77192 | tf_op jit(solution)/shard_map/while/body/eval_jaxpr/ppermute | solution.py:17
  (75 other events, 487.7 us)
where the time goes:
time: 557 us; the launch traced here: 554 us
  starting transfers between devices  312 us (56%)
  waiting for transfers between devices  113 us (20%)
  other arithmetic  86.8 us (16%)
  matrix products  15.4 us (3%)
  blocking collectives  14.2 us (3%)
  local copies, waits for them, and re-layouts  8.81 us (2%)
    ppermute x48, starting transfers between devices, extended(): before = lax.ppermute(last, axis, up)  221 us
    ppermute x48, waiting for transfers between devices, extended(): before = lax.ppermute(last, axis, up)  108 us
    ppermute x48, starting transfers between devices, extended(): after = lax.ppermute(initial, axis, down)  86.8 us
    select_n x72, other arithmetic, clip_domain(): return jnp.where(keep, field, 0.0)  49.1 us
    dot_general x80, matrix products, coefficients(): jnp.einsum('cij,fcp->fpij', onehot, table_part[:, :, :, degree], precisio...  15.4 us
    all_to_all x1, blocking collectives, body(): lax.all_to_all(image, 'depth', split_axis=0, concat_axis=2, tiled=True)  14.2 us
  transfers between devices with their start and end apart: 97, of which 41 were waited for; matrix products, arithmetic and copies ran while one was open for 3% of the time, Pallas kernels for 0%

commit v1 on v0

--- a/solution.py
+++ b/solution.py
@@ -5,6 +5,16 @@
 
 PASSES = 9
 CLASSES = 8
+
+
+def samples_point(original):
+    a_next = jnp.concatenate(
+        jax.lax.all_to_all(
+            jnp.stack(jnp.split(original, jax.lax.axis_size("depth"), axis=0)), "depth", 0, 0
+        ),
+        axis=2,
+    )
+    return a_next
 
 
 def extended(shard, sides, width):
@@ -135,7 +145,7 @@
 
     initial = (fields, jnp.zeros((velocity.shape[0], velocity.shape[1], col_count), jnp.float32))
     fields, image = lax.fori_loop(0, velocity.shape[0], descend, initial)
-    return lax.all_to_all(image, "depth", split_axis=0, concat_axis=2, tiled=True)
+    return samples_point(image)
 
 
 def solution(mesh):

time: 557 us -> 557 us (level)
  no operation moved by 1% of the time
where the time goes in v1:
time: 557 us; the launch traced here: 554 us
  starting transfers between devices  312 us (56%)
  waiting for transfers between devices  113 us (20%)
  other arithmetic  86.8 us (16%)
  matrix products  15.4 us (3%)
  blocking collectives  14.2 us (3%)
  local copies, waits for them, and re-layouts  8.83 us (2%)
    ppermute x48, starting transfers between devices, extended(): before = lax.ppermute(last, axis, up)  221 us
    ppermute x48, waiting for transfers between devices, extended(): before = lax.ppermute(last, axis, up)  108 us
    ppermute x48, starting transfers between devices, extended(): after = lax.ppermute(initial, axis, down)  86.8 us
    select_n x72, other arithmetic, clip_domain(): return jnp.where(keep, field, 0.0)  49.1 us
    dot_general x80, matrix products, coefficients(): jnp.einsum('cij,fcp->fpij', onehot, table_part[:, :, :, degree], precisio...  15.4 us
    all_to_all x1, blocking collectives, samples_point(): jax.lax.all_to_all(jnp.stack(jnp.split(original, jax.lax.axis_size('depth...  14.2 us
  transfers between devices with their start and end apart: 97, of which 41 were waited for; matrix products, arithmetic and copies ran while one was open for 3% of the time, Pallas kernels for 0%

profile of v1, /device:TPU:24, one launch (start us, length us, event | category | flops | bytes accessed | tf_op | source)
XLA Modules:
  0.0 554.2 jit_solution(2505491088299950112)
XLA Ops:
  16.5 522.7 %while.19 = (s32[]{:T(128)}, f32[2,4,16,128]{3,1,0,2:T(4,128)S(1)}, f32[8,16,128]{2,1,0:T(8,128)S(1)}, s32[8,16,128]{2,0,1:T(8,128)S(1)}, f32[2,8,2,10]{1,2,0,3:...) while((s32[]{:T(128)}, f32[2,4,16,128]{3,1,0,2:T(4,128)S(1)}, ...), condition=%wide.region_1.2_spmd.clone, body=%wide.region_0.1_spmd.clone.sunk | while | flops 12695103 | bytes 9011121 | solution.py:147
  22.6 11.6 %collective-permute-start.2 = (f32[1,2,4,3,134]{4,2,1,3,0:T(4,128)S(1)}, f32[1,2,4,3,134]{4,2,1,3,0:T(4,128)S(1)}, u32[]{:S(2)}, u32[]{:S(2)}) collective-permute-start(f32[1,2,4,3,134]{4,2,1,3,0:T(4,128)S(1)} %get-tuple-element.279), channel_id=1, source_target_pairs={{1,0},{2,1},{3,2},{4,3},{5,4},{6,5},{7,6},{8,7},{9,8},{10,9},{11,1... | collective-permute-start | bytes 38600 | tf_op jit(solution)/shard_map/while/body/eval_jaxpr/ppermute | solution.py:28
  36.2 5.8 %collective-permute-done.3 = f32[1,2,4,3,134]{4,2,1,3,0:T(4,128)S(1)} collective-permute-done((f32[1,2,4,3,134]{4,2,1,3,0:T(4,128)S(1)}, f32[1,2,4,3,134]{4,2,1,3,0:T(4,128)S(1)}, u32[]{:S(2)}, u32[]{:S(2)}) %collective-permute-start.3) | collective-permute-done | bytes 12896 | tf_op jit(solution)/shard_map/while/body/eval_jaxpr/ppermute | solution.py:27
  64.2 5.2 collective-permute-start.9
  87.1 5.9 %collective-permute-start.1 = (f32[1,2,4,16,3]{4,2,1,3,0:T(4,128)S(1)}, f32[1,2,4,16,3]{4,2,1,3,0:T(4,128)S(1)}, u32[]{:S(2)}, u32[]{:S(2)}) collective-permute-start(f32[1,2,4,16,3]{4,2,1,3,0:T(4,128)S(1)} %get-tuple-element.278), channel_id=1, source_target_pairs={{0,64},{64,128},{128,192},{192,256},{256,320},{320,384},{384,448},... | collective-permute-start | bytes 4616 | tf_op jit(solution)/shard_map/while/body/eval_jaxpr/ppermute | solution.py:27
  128.3 5.9 %collective-permute-start.9 = (f32[2,2,4,16,3]{4,2,1,3,0:T(4,128)S(1)}, f32[2,2,4,16,3]{4,2,1,3,0:T(4,128)S(1)}, u32[]{:S(2)}, u32[]{:S(2)}) collective-permute-start(f32[2,2,4,16,3]{4,2,1,3,0:T(4,128)S(1)} %get-tuple-element.288), channel_id=1, source_target_pairs={{0,64},{64,128},{128,192},{192,256},{256,320},{320,384},{384,448},... | collective-permute-start | bytes 9224 | tf_op jit(solution)/shard_map/while/body/eval_jaxpr/ppermute | solution.py:27
  151.9 5.9 %collective-permute-start.1 = (f32[1,2,4,16,3]{4,2,1,3,0:T(4,128)S(1)}, f32[1,2,4,16,3]{4,2,1,3,0:T(4,128)S(1)}, u32[]{:S(2)}, u32[]{:S(2)}) collective-permute-start(f32[1,2,4,16,3]{4,2,1,3,0:T(4,128)S(1)} %get-tuple-element.278), channel_id=1, source_target_pairs={{0,64},{64,128},{128,192},{192,256},{256,320},{320,384},{384,448},... | collective-permute-start | bytes 4616 | tf_op jit(solution)/shard_map/while/body/eval_jaxpr/ppermute | solution.py:27
  173.2 5.0 collective-permute-start.5
  193.1 5.9 %collective-permute-start.9 = (f32[2,2,4,16,3]{4,2,1,3,0:T(4,128)S(1)}, f32[2,2,4,16,3]{4,2,1,3,0:T(4,128)S(1)}, u32[]{:S(2)}, u32[]{:S(2)}) collective-permute-start(f32[2,2,4,16,3]{4,2,1,3,0:T(4,128)S(1)} %get-tuple-element.288), channel_id=1, source_target_pairs={{0,64},{64,128},{128,192},{192,256},{256,320},{320,384},{384,448},... | collective-permute-start | bytes 9224 | tf_op jit(solution)/shard_map/while/body/eval_jaxpr/ppermute | solution.py:27
  216.7 5.9 %collective-permute-start.1 = (f32[1,2,4,16,3]{4,2,1,3,0:T(4,128)S(1)}, f32[1,2,4,16,3]{4,2,1,3,0:T(4,128)S(1)}, u32[]{:S(2)}, u32[]{:S(2)}) collective-permute-start(f32[1,2,4,16,3]{4,2,1,3,0:T(4,128)S(1)} %get-tuple-element.278), channel_id=1, source_target_pairs={{0,64},{64,128},{128,192},{192,256},{256,320},{320,384},{384,448},... | collective-permute-start | bytes 4616 | tf_op jit(solution)/shard_map/while/body/eval_jaxpr/ppermute | solution.py:27
  238.0 5.0 collective-permute-start.5
  257.9 5.9 %collective-permute-start.9 = (f32[2,2,4,16,3]{4,2,1,3,0:T(4,128)S(1)}, f32[2,2,4,16,3]{4,2,1,3,0:T(4,128)S(1)}, u32[]{:S(2)}, u32[]{:S(2)}) collective-permute-start(f32[2,2,4,16,3]{4,2,1,3,0:T(4,128)S(1)} %get-tuple-element.288), channel_id=1, source_target_pairs={{0,64},{64,128},{128,192},{192,256},{256,320},{320,384},{384,448},... | collective-permute-start | bytes 9224 | tf_op jit(solution)/shard_map/while/body/eval_jaxpr/ppermute | solution.py:27
  281.5 5.9 %collective-permute-start.1 = (f32[1,2,4,16,3]{4,2,1,3,0:T(4,128)S(1)}, f32[1,2,4,16,3]{4,2,1,3,0:T(4,128)S(1)}, u32[]{:S(2)}, u32[]{:S(2)}) collective-permute-start(f32[1,2,4,16,3]{4,2,1,3,0:T(4,128)S(1)} %get-tuple-element.278), channel_id=1, source_target_pairs={{0,64},{64,128},{128,192},{192,256},{256,320},{320,384},{384,448},... | collective-permute-start | bytes 4616 | tf_op jit(solution)/shard_map/while/body/eval_jaxpr/ppermute | solution.py:27
  302.8 5.0 collective-permute-start.5
  322.7 5.9 %collective-permute-start.9 = (f32[2,2,4,16,3]{4,2,1,3,0:T(4,128)S(1)}, f32[2,2,4,16,3]{4,2,1,3,0:T(4,128)S(1)}, u32[]{:S(2)}, u32[]{:S(2)}) collective-permute-start(f32[2,2,4,16,3]{4,2,1,3,0:T(4,128)S(1)} %get-tuple-element.288), channel_id=1, source_target_pairs={{0,64},{64,128},{128,192},{192,256},{256,320},{320,384},{384,448},... | collective-permute-start | bytes 9224 | tf_op jit(solution)/shard_map/while/body/eval_jaxpr/ppermute | solution.py:27
  346.3 5.9 %collective-permute-start.1 = (f32[1,2,4,16,3]{4,2,1,3,0:T(4,128)S(1)}, f32[1,2,4,16,3]{4,2,1,3,0:T(4,128)S(1)}, u32[]{:S(2)}, u32[]{:S(2)}) collective-permute-start(f32[1,2,4,16,3]{4,2,1,3,0:T(4,128)S(1)} %get-tuple-element.278), channel_id=1, source_target_pairs={{0,64},{64,128},{128,192},{192,256},{256,320},{320,384},{384,448},... | collective-permute-start | bytes 4616 | tf_op jit(solution)/shard_map/while/body/eval_jaxpr/ppermute | solution.py:27
  367.6 5.0 collective-permute-start.5
  387.5 5.9 %collective-permute-start.9 = (f32[2,2,4,16,3]{4,2,1,3,0:T(4,128)S(1)}, f32[2,2,4,16,3]{4,2,1,3,0:T(4,128)S(1)}, u32[]{:S(2)}, u32[]{:S(2)}) collective-permute-start(f32[2,2,4,16,3]{4,2,1,3,0:T(4,128)S(1)} %get-tuple-element.288), channel_id=1, source_target_pairs={{0,64},{64,128},{128,192},{192,256},{256,320},{320,384},{384,448},... | collective-permute-start | bytes 9224 | tf_op jit(solution)/shard_map/while/body/eval_jaxpr/ppermute | solution.py:27
  411.0 5.9 %collective-permute-start.1 = (f32[1,2,4,16,3]{4,2,1,3,0:T(4,128)S(1)}, f32[1,2,4,16,3]{4,2,1,3,0:T(4,128)S(1)}, u32[]{:S(2)}, u32[]{:S(2)}) collective-permute-start(f32[1,2,4,16,3]{4,2,1,3,0:T(4,128)S(1)} %get-tuple-element.278), channel_id=1, source_target_pairs={{0,64},{64,128},{128,192},{192,256},{256,320},{320,384},{384,448},... | collective-permute-start | bytes 4616 | tf_op jit(solution)/shard_map/while/body/eval_jaxpr/ppermute | solution.py:27
  452.3 5.9 %collective-permute-start.9 = (f32[2,2,4,16,3]{4,2,1,3,0:T(4,128)S(1)}, f32[2,2,4,16,3]{4,2,1,3,0:T(4,128)S(1)}, u32[]{:S(2)}, u32[]{:S(2)}) collective-permute-start(f32[2,2,4,16,3]{4,2,1,3,0:T(4,128)S(1)} %get-tuple-element.288), channel_id=1, source_target_pairs={{0,64},{64,128},{128,192},{192,256},{256,320},{320,384},{384,448},... | collective-permute-start | bytes 9224 | tf_op jit(solution)/shard_map/while/body/eval_jaxpr/ppermute | solution.py:27
  475.8 5.9 %collective-permute-start.1 = (f32[1,2,4,16,3]{4,2,1,3,0:T(4,128)S(1)}, f32[1,2,4,16,3]{4,2,1,3,0:T(4,128)S(1)}, u32[]{:S(2)}, u32[]{:S(2)}) collective-permute-start(f32[1,2,4,16,3]{4,2,1,3,0:T(4,128)S(1)} %get-tuple-element.278), channel_id=1, source_target_pairs={{0,64},{64,128},{128,192},{192,256},{256,320},{320,384},{384,448},... | collective-permute-start | bytes 4616 | tf_op jit(solution)/shard_map/while/body/eval_jaxpr/ppermute | solution.py:27
  497.2 5.0 collective-permute-start.5
  517.1 5.9 %collective-permute-start.9 = (f32[2,2,4,16,3]{4,2,1,3,0:T(4,128)S(1)}, f32[2,2,4,16,3]{4,2,1,3,0:T(4,128)S(1)}, u32[]{:S(2)}, u32[]{:S(2)}) collective-permute-start(f32[2,2,4,16,3]{4,2,1,3,0:T(4,128)S(1)} %get-tuple-element.288), channel_id=1, source_target_pairs={{0,64},{64,128},{128,192},{192,256},{256,320},{320,384},{384,448},... | collective-permute-start | bytes 9224 | tf_op jit(solution)/shard_map/while/body/eval_jaxpr/ppermute | solution.py:27
  539.3 14.2 %all_to_all.23 = f32[8,1,16,128]{3,2,1,0:T(8,128)S(1)} all-to-all(f32[8,1,16,128]{3,2,1,0:T(8,128)S(1)} %constant_dynamic-update-slice_fusion.1), channel_id=1, replica_groups=mesh['depth'=8,'strip'=64] {'depth'}, dimensions={0} | all-to-all | bytes 131072 | tf_op jit(solution)/shard_map/all_to_all | solution.py:12
  (548 shorter events, 405.7 us)
Async XLA Ops:
  4.6 9.9 %all-to-all-start = ((s32[8,1,2048]{2,1,0:T(1,128)}), s32[8,1,2048]{2,1,0:T(1,128)S(1)}, u32[]{:S(2)}, u32[]{:S(2)}) async-start(s32[8,1,2048]{2,1,0:T(1,128)} %reshape.222), calls=%async_computation | async-start | bytes 131072 | tf_op jit(solution)/shard_map/all_to_all | solution.py:134
  22.6 13.6 %collective-permute-start.2 = (f32[1,2,4,3,134]{4,2,1,3,0:T(4,128)S(1)}, f32[1,2,4,3,134]{4,2,1,3,0:T(4,128)S(1)}, u32[]{:S(2)}, u32[]{:S(2)}) collective-permute-start(f32[1,2,4,3,134]{4,2,1,3,0:T(4,128)S(1)} %get-tuple-element.279), channel_id=1, source_target_pairs={{1,0},{2,1},{3,2},{4,3},{5,4},{6,5},{7,6},{8,7},{9,8},{10,9},{11,1... | collective-permute-start | bytes 38600 | tf_op jit(solution)/shard_map/while/body/eval_jaxpr/ppermute | solution.py:28
  52.3 8.1 %collective-permute-start.7 = (f32[2,2,4,3,134]{4,2,1,3,0:T(4,128)S(1)}, f32[2,2,4,3,134]{4,2,1,3,0:T(4,128)S(1)}, u32[]{:S(2)}, u32[]{:S(2)}) collective-permute-start(f32[2,2,4,3,134]{4,2,1,3,0:T(4,128)S(1)} %get-tuple-element.286), channel_id=1, source_target_pairs={{0,1},{1,2},{2,3},{3,4},{4,5},{5,6},{6,7},{7,8},{8,9},{9,10},{10,1... | collective-permute-start | bytes 77192 | tf_op jit(solution)/shard_map/while/body/eval_jaxpr/ppermute | solution.py:27
  72.4 8.1 %collective-permute-start.11 = (f32[2,2,4,3,134]{4,2,1,3,0:T(4,128)S(1)}, f32[2,2,4,3,134]{4,2,1,3,0:T(4,128)S(1)}, u32[]{:S(2)}, u32[]{:S(2)}) collective-permute-start(f32[2,2,4,3,134]{4,2,1,3,0:T(4,128)S(1)} %get-tuple-element.290), channel_id=1, source_target_pairs={{0,1},{1,2},{2,3},{3,4},{4,5},{5,6},{6,7},{7,8},{8,9},{9,10},{10,1... | collective-permute-start | bytes 77192 | tf_op jit(solution)/shard_map/while/body/eval_jaxpr/ppermute | solution.py:27
  85.8 8.5 %collective-permute-start = (f32[1,2,4,16,3]{4,2,1,3,0:T(4,128)S(1)}, f32[1,2,4,16,3]{4,2,1,3,0:T(4,128)S(1)}, u32[]{:S(2)}, u32[]{:S(2)}) collective-permute-start(f32[1,2,4,16,3]{4,2,1,3,0:T(4,128)S(1)} %get-tuple-element.277), channel_id=1, source_target_pairs={{64,0},{128,64},{192,128},{256,192},{320,256},{384,320},{448,384},... | collective-permute-start | bytes 4616 | tf_op jit(solution)/shard_map/while/body/eval_jaxpr/ppermute | solution.py:28
  116.5 8.1 %collective-permute-start.7 = (f32[2,2,4,3,134]{4,2,1,3,0:T(4,128)S(1)}, f32[2,2,4,3,134]{4,2,1,3,0:T(4,128)S(1)}, u32[]{:S(2)}, u32[]{:S(2)}) collective-permute-start(f32[2,2,4,3,134]{4,2,1,3,0:T(4,128)S(1)} %get-tuple-element.286), channel_id=1, source_target_pairs={{0,1},{1,2},{2,3},{3,4},{4,5},{5,6},{6,7},{7,8},{8,9},{9,10},{10,1... | collective-permute-start | bytes 77192 | tf_op jit(solution)/shard_map/while/body/eval_jaxpr/ppermute | solution.py:27
  137.2 8.1 %collective-permute-start.11 = (f32[2,2,4,3,134]{4,2,1,3,0:T(4,128)S(1)}, f32[2,2,4,3,134]{4,2,1,3,0:T(4,128)S(1)}, u32[]{:S(2)}, u32[]{:S(2)}) collective-permute-start(f32[2,2,4,3,134]{4,2,1,3,0:T(4,128)S(1)} %get-tuple-element.290), channel_id=1, source_target_pairs={{0,1},{1,2},{2,3},{3,4},{4,5},{5,6},{6,7},{7,8},{8,9},{9,10},{10,1... | collective-permute-start | bytes 77192 | tf_op jit(solution)/shard_map/while/body/eval_jaxpr/ppermute | solution.py:27
  150.6 8.5 %collective-permute-start = (f32[1,2,4,16,3]{4,2,1,3,0:T(4,128)S(1)}, f32[1,2,4,16,3]{4,2,1,3,0:T(4,128)S(1)}, u32[]{:S(2)}, u32[]{:S(2)}) collective-permute-start(f32[1,2,4,16,3]{4,2,1,3,0:T(4,128)S(1)} %get-tuple-element.277), channel_id=1, source_target_pairs={{64,0},{128,64},{192,128},{256,192},{320,256},{384,320},{448,384},... | collective-permute-start | bytes 4616 | tf_op jit(solution)/shard_map/while/body/eval_jaxpr/ppermute | solution.py:28
  181.3 8.1 %collective-permute-start.7 = (f32[2,2,4,3,134]{4,2,1,3,0:T(4,128)S(1)}, f32[2,2,4,3,134]{4,2,1,3,0:T(4,128)S(1)}, u32[]{:S(2)}, u32[]{:S(2)}) collective-permute-start(f32[2,2,4,3,134]{4,2,1,3,0:T(4,128)S(1)} %get-tuple-element.286), channel_id=1, source_target_pairs={{0,1},{1,2},{2,3},{3,4},{4,5},{5,6},{6,7},{7,8},{8,9},{9,10},{10,1... | collective-permute-start | bytes 77192 | tf_op jit(solution)/shard_map/while/body/eval_jaxpr/ppermute | solution.py:27
  202.0 8.1 %collective-permute-start.11 = (f32[2,2,4,3,134]{4,2,1,3,0:T(4,128)S(1)}, f32[2,2,4,3,134]{4,2,1,3,0:T(4,128)S(1)}, u32[]{:S(2)}, u32[]{:S(2)}) collective-permute-start(f32[2,2,4,3,134]{4,2,1,3,0:T(4,128)S(1)} %get-tuple-element.290), channel_id=1, source_target_pairs={{0,1},{1,2},{2,3},{3,4},{4,5},{5,6},{6,7},{7,8},{8,9},{9,10},{10,1... | collective-permute-start | bytes 77192 | tf_op jit(solution)/shard_map/while/body/eval_jaxpr/ppermute | solution.py:27
  215.4 8.5 %collective-permute-start = (f32[1,2,4,16,3]{4,2,1,3,0:T(4,128)S(1)}, f32[1,2,4,16,3]{4,2,1,3,0:T(4,128)S(1)}, u32[]{:S(2)}, u32[]{:S(2)}) collective-permute-start(f32[1,2,4,16,3]{4,2,1,3,0:T(4,128)S(1)} %get-tuple-element.277), channel_id=1, source_target_pairs={{64,0},{128,64},{192,128},{256,192},{320,256},{384,320},{448,384},... | collective-permute-start | bytes 4616 | tf_op jit(solution)/shard_map/while/body/eval_jaxpr/ppermute | solution.py:28
  246.1 8.1 %collective-permute-start.7 = (f32[2,2,4,3,134]{4,2,1,3,0:T(4,128)S(1)}, f32[2,2,4,3,134]{4,2,1,3,0:T(4,128)S(1)}, u32[]{:S(2)}, u32[]{:S(2)}) collective-permute-start(f32[2,2,4,3,134]{4,2,1,3,0:T(4,128)S(1)} %get-tuple-element.286), channel_id=1, source_target_pairs={{0,1},{1,2},{2,3},{3,4},{4,5},{5,6},{6,7},{7,8},{8,9},{9,10},{10,1... | collective-permute-start | bytes 77192 | tf_op jit(solution)/shard_map/while/body/eval_jaxpr/ppermute | solution.py:27
  266.8 8.1 %collective-permute-start.11 = (f32[2,2,4,3,134]{4,2,1,3,0:T(4,128)S(1)}, f32[2,2,4,3,134]{4,2,1,3,0:T(4,128)S(1)}, u32[]{:S(2)}, u32[]{:S(2)}) collective-permute-start(f32[2,2,4,3,134]{4,2,1,3,0:T(4,128)S(1)} %get-tuple-element.290), channel_id=1, source_target_pairs={{0,1},{1,2},{2,3},{3,4},{4,5},{5,6},{6,7},{7,8},{8,9},{9,10},{10,1... | collective-permute-start | bytes 77192 | tf_op jit(solution)/shard_map/while/body/eval_jaxpr/ppermute | solution.py:27
  280.2 8.5 %collective-permute-start = (f32[1,2,4,16,3]{4,2,1,3,0:T(4,128)S(1)}, f32[1,2,4,16,3]{4,2,1,3,0:T(4,128)S(1)}, u32[]{:S(2)}, u32[]{:S(2)}) collective-permute-start(f32[1,2,4,16,3]{4,2,1,3,0:T(4,128)S(1)} %get-tuple-element.277), channel_id=1, source_target_pairs={{64,0},{128,64},{192,128},{256,192},{320,256},{384,320},{448,384},... | collective-permute-start | bytes 4616 | tf_op jit(solution)/shard_map/while/body/eval_jaxpr/ppermute | solution.py:28
  310.9 8.1 %collective-permute-start.7 = (f32[2,2,4,3,134]{4,2,1,3,0:T(4,128)S(1)}, f32[2,2,4,3,134]{4,2,1,3,0:T(4,128)S(1)}, u32[]{:S(2)}, u32[]{:S(2)}) collective-permute-start(f32[2,2,4,3,134]{4,2,1,3,0:T(4,128)S(1)} %get-tuple-element.286), channel_id=1, source_target_pairs={{0,1},{1,2},{2,3},{3,4},{4,5},{5,6},{6,7},{7,8},{8,9},{9,10},{10,1... | collective-permute-start | bytes 77192 | tf_op jit(solution)/shard_map/while/body/eval_jaxpr/ppermute | solution.py:27
  331.6 8.1 %collective-permute-start.11 = (f32[2,2,4,3,134]{4,2,1,3,0:T(4,128)S(1)}, f32[2,2,4,3,134]{4,2,1,3,0:T(4,128)S(1)}, u32[]{:S(2)}, u32[]{:S(2)}) collective-permute-start(f32[2,2,4,3,134]{4,2,1,3,0:T(4,128)S(1)} %get-tuple-element.290), channel_id=1, source_target_pairs={{0,1},{1,2},{2,3},{3,4},{4,5},{5,6},{6,7},{7,8},{8,9},{9,10},{10,1... | collective-permute-start | bytes 77192 | tf_op jit(solution)/shard_map/while/body/eval_jaxpr/ppermute | solution.py:27
  345.0 8.5 %collective-permute-start = (f32[1,2,4,16,3]{4,2,1,3,0:T(4,128)S(1)}, f32[1,2,4,16,3]{4,2,1,3,0:T(4,128)S(1)}, u32[]{:S(2)}, u32[]{:S(2)}) collective-permute-start(f32[1,2,4,16,3]{4,2,1,3,0:T(4,128)S(1)} %get-tuple-element.277), channel_id=1, source_target_pairs={{64,0},{128,64},{192,128},{256,192},{320,256},{384,320},{448,384},... | collective-permute-start | bytes 4616 | tf_op jit(solution)/shard_map/while/body/eval_jaxpr/ppermute | solution.py:28
  396.4 8.1 %collective-permute-start.11 = (f32[2,2,4,3,134]{4,2,1,3,0:T(4,128)S(1)}, f32[2,2,4,3,134]{4,2,1,3,0:T(4,128)S(1)}, u32[]{:S(2)}, u32[]{:S(2)}) collective-permute-start(f32[2,2,4,3,134]{4,2,1,3,0:T(4,128)S(1)} %get-tuple-element.290), channel_id=1, source_target_pairs={{0,1},{1,2},{2,3},{3,4},{4,5},{5,6},{6,7},{7,8},{8,9},{9,10},{10,1... | collective-permute-start | bytes 77192 | tf_op jit(solution)/shard_map/while/body/eval_jaxpr/ppermute | solution.py:27
  409.7 8.5 %collective-permute-start = (f32[1,2,4,16,3]{4,2,1,3,0:T(4,128)S(1)}, f32[1,2,4,16,3]{4,2,1,3,0:T(4,128)S(1)}, u32[]{:S(2)}, u32[]{:S(2)}) collective-permute-start(f32[1,2,4,16,3]{4,2,1,3,0:T(4,128)S(1)} %get-tuple-element.277), channel_id=1, source_target_pairs={{64,0},{128,64},{192,128},{256,192},{320,256},{384,320},{448,384},... | collective-permute-start | bytes 4616 | tf_op jit(solution)/shard_map/while/body/eval_jaxpr/ppermute | solution.py:28
  440.4 8.1 %collective-permute-start.7 = (f32[2,2,4,3,134]{4,2,1,3,0:T(4,128)S(1)}, f32[2,2,4,3,134]{4,2,1,3,0:T(4,128)S(1)}, u32[]{:S(2)}, u32[]{:S(2)}) collective-permute-start(f32[2,2,4,3,134]{4,2,1,3,0:T(4,128)S(1)} %get-tuple-element.286), channel_id=1, source_target_pairs={{0,1},{1,2},{2,3},{3,4},{4,5},{5,6},{6,7},{7,8},{8,9},{9,10},{10,1... | collective-permute-start | bytes 77192 | tf_op jit(solution)/shard_map/while/body/eval_jaxpr/ppermute | solution.py:27
  461.2 8.1 %collective-permute-start.11 = (f32[2,2,4,3,134]{4,2,1,3,0:T(4,128)S(1)}, f32[2,2,4,3,134]{4,2,1,3,0:T(4,128)S(1)}, u32[]{:S(2)}, u32[]{:S(2)}) collective-permute-start(f32[2,2,4,3,134]{4,2,1,3,0:T(4,128)S(1)} %get-tuple-element.290), channel_id=1, source_target_pairs={{0,1},{1,2},{2,3},{3,4},{4,5},{5,6},{6,7},{7,8},{8,9},{9,10},{10,1... | collective-permute-start | bytes 77192 | tf_op jit(solution)/shard_map/while/body/eval_jaxpr/ppermute | solution.py:27
  474.5 8.5 %collective-permute-start = (f32[1,2,4,16,3]{4,2,1,3,0:T(4,128)S(1)}, f32[1,2,4,16,3]{4,2,1,3,0:T(4,128)S(1)}, u32[]{:S(2)}, u32[]{:S(2)}) collective-permute-start(f32[1,2,4,16,3]{4,2,1,3,0:T(4,128)S(1)} %get-tuple-element.277), channel_id=1, source_target_pairs={{64,0},{128,64},{192,128},{256,192},{320,256},{384,320},{448,384},... | collective-permute-start | bytes 4616 | tf_op jit(solution)/shard_map/while/body/eval_jaxpr/ppermute | solution.py:28
  505.2 8.1 %collective-permute-start.7 = (f32[2,2,4,3,134]{4,2,1,3,0:T(4,128)S(1)}, f32[2,2,4,3,134]{4,2,1,3,0:T(4,128)S(1)}, u32[]{:S(2)}, u32[]{:S(2)}) collective-permute-start(f32[2,2,4,3,134]{4,2,1,3,0:T(4,128)S(1)} %get-tuple-element.286), channel_id=1, source_target_pairs={{0,1},{1,2},{2,3},{3,4},{4,5},{5,6},{6,7},{7,8},{8,9},{9,10},{10,1... | collective-permute-start | bytes 77192 | tf_op jit(solution)/shard_map/while/body/eval_jaxpr/ppermute | solution.py:27
  526.0 8.1 %collective-permute-start.11 = (f32[2,2,4,3,134]{4,2,1,3,0:T(4,128)S(1)}, f32[2,2,4,3,134]{4,2,1,3,0:T(4,128)S(1)}, u32[]{:S(2)}, u32[]{:S(2)}) collective-permute-start(f32[2,2,4,3,134]{4,2,1,3,0:T(4,128)S(1)} %get-tuple-element.290), channel_id=1, source_target_pairs={{0,1},{1,2},{2,3},{3,4},{4,5},{5,6},{6,7},{7,8},{8,9},{9,10},{10,1... | collective-permute-start | bytes 77192 | tf_op jit(solution)/shard_map/while/body/eval_jaxpr/ppermute | solution.py:27
  (75 other events, 487.7 us)
